TPU v7x, 128 devices: a whole 4x4x4 slice. The times are simulated.
128 devices in a mesh: grp: 4 (over z), list: 32 (over y, x, core).
Axes of the slice: x: 4, y: 4, z: 4, core: 2. Of those that a mesh axis runs over, the one named last changes fastest.
Arguments:
- vectors: bfloat16 [3, 65536, 1024], P(None, ('grp', 'list')), may hold values from -6 to 6
- owner_route: int32 [3, 65536, 1], P(None, ('grp', 'list')), may hold values from 0 to 31; in each aligned block of 512 rows (0 to 511, 512 to 1023, ..., all dimensions but the last counted through in order) at most 32 rows name the same one
- list_slot: int32 [3, 65536], P(None, ('grp', 'list')), may hold values from 0 to 1023
- centroids: float32 [32768, 1024], P('list'), may hold values from -6 to 6
- counts: int32 [32768], P('list'), may hold values from 1 to 8
Outputs:
- residuals: bfloat16 [3, 65536, 1024], P(None, ('grp', 'list'))
- new_centroids: float32 [32768, 1024], P('list')
Inputs may be any that keep to these rules, and one draw needn't show every extreme that they name: `owner_route`: within the rows of one device for one step, at most 32 vectors name the same owner; some owner is named exactly 32 times.
All inputs are finite; a program needn't handle non-finite values.
Results may differ from a plain program's by a relative error of at most 0.0035.
Values may be sent and summed in bfloat16 or wider, within the bound.
No kernel may reach another device: no remote copies, remote signals or barrier semaphores. Data moves between devices by JAX's collectives and lax.ppermute only.
A program may use at most 128 MiB of HBM per device.

v0:
```python
import jax
import jax.numpy as jnp
from jax import lax
from jax.sharding import PartitionSpec as P

STEPS = 3


def list_sums(slots, rows, list_dev):
    one_hot = (jnp.arange(list_dev, dtype=jnp.int32)[:, None] == slots[None, :]).astype(
        jnp.bfloat16
    )
    sums = jnp.dot(one_hot, rows, preferred_element_type=jnp.float32)
    return (sums, jnp.sum(one_hot, axis=1, dtype=jnp.float32))


def local(vectors, owner_route, list_slot, centroids, counts):
    owner_count = lax.axis_size("list")
    row_count = vectors.shape[1]
    width = vectors.shape[2]
    capacity = 2 * row_count // owner_count
    list_dev = centroids.shape[0]
    current = centroids
    weights = counts.astype(jnp.float32)
    outputs = []
    for step_index in range(STEPS):
        owner_ids = owner_route[step_index, :, 0]
        slot_ids = list_slot[step_index]
        owner_hits = (
            owner_ids[:, None] == jnp.arange(owner_count, dtype=jnp.int32)[None, :]
        ).astype(jnp.int32)
        rank_rows = jnp.sum((jnp.cumsum(owner_hits, axis=0) - owner_hits) * owner_hits, axis=1)
        dest_rows = owner_ids * capacity + rank_rows
        send_rows = (
            jnp.zeros((owner_count * capacity, width), jnp.bfloat16)
            .at[dest_rows]
            .set(vectors[step_index])
        )
        send_rows = send_rows.reshape(owner_count, capacity, width)
        send_slots = jnp.full((owner_count * capacity,), -1, jnp.int32).at[dest_rows].set(slot_ids)
        send_slots = send_slots.reshape(owner_count, capacity)
        table = current

        def route_fn(pieces, table=table):
            vec_rows, list_ids = pieces
            chosen = table[jnp.clip(list_ids, 0, list_dev - 1)]
            residual_rows = (vec_rows.astype(jnp.float32) - chosen).astype(jnp.bfloat16)
            back_rows = lax.all_to_all(
                residual_rows, "list", split_axis=0, concat_axis=0, tiled=True
            )
            return (back_rows, vec_rows, list_ids)

        back_rows, recv_rows, recv_slots = route_fn(
            (
                lax.all_to_all(send_rows, "list", split_axis=0, concat_axis=0, tiled=True),
                lax.all_to_all(send_slots, "list", split_axis=0, concat_axis=0, tiled=True),
            )
        )
        outputs.append(back_rows.reshape(owner_count * capacity, width)[dest_rows])
        flat_rows = recv_rows.reshape(-1, width)
        flat_slots = recv_slots.reshape(-1)
        sums, batch_count = list_sums(flat_slots, flat_rows, list_dev)
        total_sums, total_count = (
            lax.psum(sums.astype(jnp.bfloat16), "grp").astype(jnp.float32),
            lax.psum(batch_count.astype(jnp.bfloat16), "grp").astype(jnp.float32),
        )
        current = (weights[:, None] * current + total_sums) / (weights + total_count)[:, None]
        weights = weights + total_count
    return (jnp.stack(outputs, axis=0), current)


def solution(mesh):
    in_specs = (
        P(None, ("grp", "list"), None),
        P(None, ("grp", "list"), None),
        P(None, ("grp", "list")),
        P("list", None),
        P("list"),
    )
    out_specs = (P(None, ("grp", "list"), None), P("list", None))
    return jax.shard_map(local, mesh=mesh, in_specs=in_specs, out_specs=out_specs, check_vma=False)
```

profile of v0, /device:TPU:0, one launch (start us, length us, event | category | flops | bytes accessed | tf_op | source)
XLA Modules:
  0.0 397.1 jit_solution(9526469417952136260)
XLA Ops:
  7.2 0.8 fusion.46
  8.0 0.7 fusion.47
  8.7 1.2 reduce-window.24
  9.9 0.2 slice_reduce_fusion.1
  10.2 1.2 reduce-window.20
  11.3 0.2 slice_reduce_fusion.2
  11.6 1.2 reduce-window.26
  12.8 0.2 slice_reduce_fusion
  13.0 0.1 fusion.32
  13.2 0.1 fusion.35
  13.3 0.1 fusion.29
  13.4 0.7 compare_select_fusion.3
  14.1 2.4 scatter_custom_fusion.3
  16.5 0.7 all_to_all.41
  17.2 7.4 %all-to-all-start.4 = ((s32[32,1,32]{2,1,0:T(1,128)}), s32[32,1,32]{2,1,0:T(1,128)S(1)}, u32[]{:S(2)}, u32[]{:S(2)}) async-start(s32[32,1,32]{2,1,0:T(1,128)} %all_to_all.41), calls=%async_computation.4 | async-start | bytes 32768 | tf_op jit(solution)/shard_map/all_to_all | solution.py:56
  24.6 2.4 scatter_custom_fusion.5
  27.1 0.7 all_to_all.45
  27.8 4.1 %all-to-all-done.4 = s32[32,1,32]{2,1,0:T(1,128)S(1)} async-done(((s32[32,1,32]{2,1,0:T(1,128)}), s32[32,1,32]{2,1,0:T(1,128)S(1)}, u32[]{:S(2)}, u32[]{:S(2)}) %all-to-all-start.4) | async-done | bytes 4128 | tf_op jit(solution)/shard_map/all_to_all | solution.py:56
  31.9 3.9 all-to-all-start.7
  35.8 2.4 scatter_custom_fusion.1
  38.2 0.7 all_to_all.37
  38.9 4.2 %all-to-all-done.7 = s32[32,1,32]{2,1,0:T(1,128)S(1)} async-done(((s32[32,1,32]{2,1,0:T(1,128)}), s32[32,1,32]{2,1,0:T(1,128)S(1)}, u32[]{:S(2)}, u32[]{:S(2)}) %all-to-all-start.7) | async-done | bytes 4128 | tf_op jit(solution)/shard_map/all_to_all | solution.py:56
  43.1 3.8 all-to-all-start.1
  47.0 4.8 %scatter_custom_fusion.2 = bf16[1024,1024]{1,0:T(8,128)(2,1)} fusion(s32[512]{0:T(512)S(1)} %bitcast.152, bf16[3,512,1024]{2,1,0:T(8,128)(2,1)} %param.5, bf16[]{:T(256)} %constant.10.clone.1), kind=kCustom, calls=%fused_computation.39 | custom fusion | bytes 3146240 | tf_op jit(solution)/shard_map/scatter | solution.py:37
  51.8 2.5 all-to-all-done.1
  54.2 4.9 %all-to-all-start.3 = ((bf16[32,32,1024]{2,1,0:T(8,128)(2,1)}), bf16[32,32,1024]{2,1,0:T(8,128)(2,1)S(1)}, u32[]{:S(2)}, u32[]{:S(2)}) async-start(bf16[32,32,1024]{2,1,0:T(8,128)(2,1)} %bitcast.22), calls=%async_computation.3 | async-start | bytes 4194304 | tf_op jit(solution)/shard_map/all_to_all | solution.py:55
  59.2 4.8 %scatter_custom_fusion.4 = bf16[1024,1024]{1,0:T(8,128)(2,1)} fusion(s32[512]{0:T(512)S(1)} %bitcast.155, bf16[3,512,1024]{2,1,0:T(8,128)(2,1)} %param.5, bf16[]{:T(256)} %constant.10.clone.1), kind=kCustom, calls=%fused_computation.37 | custom fusion | bytes 3146240 | tf_op jit(solution)/shard_map/scatter | solution.py:37
  64.0 25.2 %all-to-all-done.3 = bf16[32,32,1024]{2,1,0:T(8,128)(2,1)S(1)} async-done(((bf16[32,32,1024]{2,1,0:T(8,128)(2,1)}), bf16[32,32,1024]{2,1,0:T(8,128)(2,1)S(1)}, u32[]{:S(2)}, u32[]{:S(2)}) %all-to-all-start.3) | async-done | bytes 2097184 | tf_op jit(solution)/shard_map/all_to_all | solution.py:55
  89.1 4.8 %all-to-all-start.6 = ((bf16[32,32,1024]{2,1,0:T(8,128)(2,1)}), bf16[32,32,1024]{2,1,0:T(8,128)(2,1)}, u32[]{:S(2)}, u32[]{:S(2)}) async-start(bf16[32,32,1024]{2,1,0:T(8,128)(2,1)} %bitcast.37), calls=%async_computation.6 | async-start | bytes 4194304 | tf_op jit(solution)/shard_map/all_to_all | solution.py:55
  93.9 4.8 %scatter_custom_fusion = bf16[1024,1024]{1,0:T(8,128)(2,1)} fusion(s32[512]{0:T(512)S(1)} %bitcast.158, bf16[3,512,1024]{2,1,0:T(8,128)(2,1)} %param.5, bf16[]{:T(256)} %constant.10.clone.1), kind=kCustom, calls=%fused_computation.41 | custom fusion | bytes 3146240 | tf_op jit(solution)/shard_map/scatter | solution.py:37
  98.7 25.2 %all-to-all-done.6 = bf16[32,32,1024]{2,1,0:T(8,128)(2,1)} async-done(((bf16[32,32,1024]{2,1,0:T(8,128)(2,1)}), bf16[32,32,1024]{2,1,0:T(8,128)(2,1)}, u32[]{:S(2)}, u32[]{:S(2)}) %all-to-all-start.6) | async-done | bytes 2097184 | tf_op jit(solution)/shard_map/all_to_all | solution.py:55
  123.9 4.8 %all-to-all-start = ((bf16[32,32,1024]{2,1,0:T(8,128)(2,1)}), bf16[32,32,1024]{2,1,0:T(8,128)(2,1)}, u32[]{:S(2)}, u32[]{:S(2)}) async-start(bf16[32,32,1024]{2,1,0:T(8,128)(2,1)} %bitcast.7), calls=%async_computation | async-start | bytes 4194304 | tf_op jit(solution)/shard_map/all_to_all | solution.py:55
  128.7 0.5 broadcast.296
  129.2 0.7 fusion.45
  129.9 0.1 eq.137
  130.0 0.7 reduce.20
  130.8 0.7 reduce.18
  131.6 3.7 fusion.13
  135.2 5.3 %fusion.14 = bf16[1024,1024]{1,0:T(8,128)(2,1)} fusion(bf16[1024,1024]{1,0:T(8,128)(2,1)} %bitcast.45, s32[1024]{0:T(1024)S(1)} %eq.153), kind=kOutput, calls=%fused_computation.36 | convolution fusion | flops 2149580800 | bytes 4198400 | tf_op jit(solution)/shard_map/dot_general | solution.py:13
  140.5 18.1 %all-to-all-done = bf16[32,32,1024]{2,1,0:T(8,128)(2,1)} async-done(((bf16[32,32,1024]{2,1,0:T(8,128)(2,1)}), bf16[32,32,1024]{2,1,0:T(8,128)(2,1)}, u32[]{:S(2)}, u32[]{:S(2)}) %all-to-all-start) | async-done | bytes 2097184 | tf_op jit(solution)/shard_map/all_to_all | solution.py:55
  158.6 5.2 %fusion.12 = bf16[1024,1024]{1,0:T(8,128)(2,1)} fusion(bf16[1024,1024]{1,0:T(8,128)(2,1)} %bitcast.23, s32[1024]{0:T(1024)S(1)} %eq.137), kind=kOutput, calls=%fused_computation.34 | convolution fusion | flops 2149580800 | bytes 4198400 | tf_op jit(solution)/shard_map/dot_general | solution.py:13
  163.8 0.7 copy-done.1
  164.5 0.1 reshape.268
  164.6 0.1 reshape.300
  164.7 8.5 %gather_fusion = f32[1024,1024]{1,0:T(8,128)} fusion(f32[1024,1024]{1,0:T(8,128)} %param.8, s32[1024]{0:T(1024)S(1)} %broadcast_clamp_fusion.2), kind=kCustom, calls=%fused_computation | custom fusion | bytes 8392704 | tf_op jit(solution)/shard_map/gather | solution.py:46
  173.2 0.5 fusion.8
  173.7 1.0 fusion.6
  174.7 12.1 %all-reduce = (bf16[1024]{0:T(1024)(128)(2,1)S(1)}, bf16[1024]{0:T(1024)(128)(2,1)S(1)}, bf16[1024]{0:T(1024)(128)(2,1)S(1)}) all-reduce(bf16[1024]{0:T(1024)(128)(2,1)S(1)} %get-tuple-element.25, bf16[1024]{0:T(1024)(128)(2,1)S(1)} %get-tuple-element.26, bf16[1024]{0:T(1024)(128)(2,1)S(1)} %fusion.8), channel_id=1, replica_groups=mesh['grp'=4,'list'=32] {'grp'}, use_global_device_ids=true, to_apply=%region_11.12 | all-reduce | flops 3072 | bytes 12288 | tf_op jit(solution)/shard_map/psum | solution.py:65
  186.9 5.1 %subtract_convert_fusion.2 = bf16[32,32,1024]{2,1,0:T(8,128)(2,1)} fusion(f32[32,32,1024]{2,1,0:T(8,128)} %bitcast.133, bf16[32,32,1024]{2,1,0:T(8,128)(2,1)} %all-to-all-done), kind=kLoop, calls=%fused_computation.26 | loop fusion | flops 3145728 | bytes 8388608 | tf_op jit(solution)/shard_map/convert_element_type | solution.py:47
  192.0 4.2 %all-to-all-start.2 = ((bf16[32,32,1024]{2,1,0:T(8,128)(2,1)}), bf16[32,32,1024]{2,1,0:T(8,128)(2,1)S(1)}, u32[]{:S(2)}, u32[]{:S(2)}) async-start(bf16[32,32,1024]{2,1,0:T(8,128)(2,1)} %subtract_convert_fusion.2), calls=%async_computation.2 | async-start | bytes 4194304 | tf_op jit(solution)/shard_map/all_to_all | solution.py:48
  196.3 93.5 %all-reduce.4.cloned.1.call-done = (bf16[1024,1024]{1,0:T(8,128)(2,1)}, bf16[1024,1024]{1,0:T(8,128)(2,1)}, bf16[1024,1024]{1,0:T(8,128)(2,1)}) async-done(((bf16[1024,1024]{1,0:T(8,128)(2,1)}, bf16[1024,1024]{1,0:T(8,128)(2,1)}, bf16[1024,1024]{1,0:T(8,128)(2,1)}), (bf16[1024,1024]{1,0:T(8,128)(2,1)}, bf16[1024,1024]{1,0:T(8,128)(2,1)}, bf16[1024,1024]{1,0:T(8,128)(2,1)})) %all-reduce.4.cloned.1.call-update) | async-done | bytes 6291472 | tf_op jit(solution)/shard_map/psum | solution.py:64
  289.7 8.4 %add_divide_fusion = (f32[1024,1024]{1,0:T(8,128)}, f32[1024,1024]{1,0:T(8,128)}, f32[1024,1024]{1,0:T(8,128)}) fusion(bf16[1024,1024]{1,0:T(8,128)(2,1)} %get-tuple-element.7, f32[1024]{0:T(1024)S(1)} %get-tuple-element.11, f32[1024]{0:T(1024)S(1)} %get-tuple-element.12, bf16[1024,1024]{1,0:T(8,128)(2,1)} %get-tuple-element.5, ...), kind=kLoop, calls=%fused_computation.12 | loop fusion | flops 12582912 | bytes 23085056 | tf_op jit(solution)/shard_map/div | solution.py:67
  298.1 8.6 %gather_fusion.4 = f32[1024,1024]{1,0:T(8,128)} fusion(f32[1024,1024]{1,0:T(8,128)} %get-tuple-element.9, s32[1024]{0:T(1024)S(1)} %broadcast_clamp_fusion), kind=kCustom, calls=%fused_computation.4 | custom fusion | bytes 8392704 | tf_op jit(solution)/shard_map/gather | solution.py:46
  306.7 5.0 %subtract_convert_fusion = bf16[32,32,1024]{2,1,0:T(8,128)(2,1)} fusion(f32[32,32,1024]{2,1,0:T(8,128)} %bitcast.134, bf16[32,32,1024]{2,1,0:T(8,128)(2,1)} %all-to-all-done.6), kind=kLoop, calls=%fused_computation.16 | loop fusion | flops 3145728 | bytes 8388608 | tf_op jit(solution)/shard_map/convert_element_type | solution.py:47
  311.7 7.2 %all-to-all-start.8 = ((bf16[32,32,1024]{2,1,0:T(8,128)(2,1)}), bf16[32,32,1024]{2,1,0:T(8,128)(2,1)}, u32[]{:S(2)}, u32[]{:S(2)}) async-start(bf16[32,32,1024]{2,1,0:T(8,128)(2,1)} %subtract_convert_fusion), calls=%async_computation.8 | async-start | bytes 4194304 | tf_op jit(solution)/shard_map/all_to_all | solution.py:48
  319.0 8.6 %gather_fusion.2 = f32[1024,1024]{1,0:T(8,128)} fusion(f32[1024,1024]{1,0:T(8,128)} %get-tuple-element.10, s32[1024]{0:T(1024)S(1)} %broadcast_clamp_fusion.1), kind=kCustom, calls=%fused_computation.2 | custom fusion | bytes 8392704 | tf_op jit(solution)/shard_map/gather | solution.py:46
  327.6 5.0 %subtract_convert_fusion.1 = bf16[32,32,1024]{2,1,0:T(8,128)(2,1)} fusion(f32[32,32,1024]{2,1,0:T(8,128)} %bitcast.135, bf16[32,32,1024]{2,1,0:T(8,128)(2,1)} %copy-done), kind=kLoop, calls=%fused_computation.21 | loop fusion | flops 3145728 | bytes 8388608 | tf_op jit(solution)/shard_map/convert_element_type | solution.py:47
  332.6 16.3 %all-to-all-done.8 = bf16[32,32,1024]{2,1,0:T(8,128)(2,1)} async-done(((bf16[32,32,1024]{2,1,0:T(8,128)(2,1)}), bf16[32,32,1024]{2,1,0:T(8,128)(2,1)}, u32[]{:S(2)}, u32[]{:S(2)}) %all-to-all-start.8) | async-done | bytes 2097184 | tf_op jit(solution)/shard_map/all_to_all | solution.py:48
  348.9 4.8 %all-to-all-start.5 = ((bf16[32,32,1024]{2,1,0:T(8,128)(2,1)}), bf16[32,32,1024]{2,1,0:T(8,128)(2,1)}, u32[]{:S(2)}, u32[]{:S(2)}) async-start(bf16[32,32,1024]{2,1,0:T(8,128)(2,1)} %subtract_convert_fusion.1), calls=%async_computation.5 | async-start | bytes 4194304 | tf_op jit(solution)/shard_map/all_to_all | solution.py:48
  353.7 2.1 gather_fusion.1
  355.8 4.6 %gather_fusion.5 = bf16[512,1024]{1,0:T(8,128)(2,1)S(1)} fusion(bf16[1024,1024]{1,0:T(8,128)(2,1)} %bitcast.43, s32[1024]{0:T(1024)S(1)} %pad_clamp_fusion), kind=kCustom, calls=%fused_computation.5 | custom fusion | bytes 2099200 | tf_op jit(solution)/shard_map/gather | solution.py:59
  360.4 23.3 %all-to-all-done.5 = bf16[32,32,1024]{2,1,0:T(8,128)(2,1)} async-done(((bf16[32,32,1024]{2,1,0:T(8,128)(2,1)}), bf16[32,32,1024]{2,1,0:T(8,128)(2,1)}, u32[]{:S(2)}, u32[]{:S(2)}) %all-to-all-start.5) | async-done | bytes 2097184 | tf_op jit(solution)/shard_map/all_to_all | solution.py:48
  383.6 4.6 %gather_fusion.3 = bf16[512,1024]{1,0:T(8,128)(2,1)S(1)} fusion(bf16[1024,1024]{1,0:T(8,128)(2,1)} %bitcast.28, s32[1024]{0:T(1024)S(1)} %pad_clamp_fusion.1), kind=kCustom, calls=%fused_computation.3 | custom fusion | bytes 2099200 | tf_op jit(solution)/shard_map/gather | solution.py:59
  388.2 2.0 pad_maximum_fusion
  (31 shorter events, 0.5 us)
Async XLA Ops:
  17.2 14.7 %all-to-all-start.4 = ((s32[32,1,32]{2,1,0:T(1,128)}), s32[32,1,32]{2,1,0:T(1,128)S(1)}, u32[]{:S(2)}, u32[]{:S(2)}) async-start(s32[32,1,32]{2,1,0:T(1,128)} %all_to_all.41), calls=%async_computation.4 | async-start | bytes 32768 | tf_op jit(solution)/shard_map/all_to_all | solution.py:56
  31.9 11.2 %all-to-all-start.7 = ((s32[32,1,32]{2,1,0:T(1,128)}), s32[32,1,32]{2,1,0:T(1,128)S(1)}, u32[]{:S(2)}, u32[]{:S(2)}) async-start(s32[32,1,32]{2,1,0:T(1,128)} %all_to_all.45), calls=%async_computation.7 | async-start | bytes 32768 | tf_op jit(solution)/shard_map/all_to_all | solution.py:56
  43.1 11.1 %all-to-all-start.1 = ((s32[32,1,32]{2,1,0:T(1,128)}), s32[32,1,32]{2,1,0:T(1,128)S(1)}, u32[]{:S(2)}, u32[]{:S(2)}) async-start(s32[32,1,32]{2,1,0:T(1,128)} %all_to_all.37), calls=%async_computation.1 | async-start | bytes 32768 | tf_op jit(solution)/shard_map/all_to_all | solution.py:56
  54.2 34.9 %all-to-all-start.3 = ((bf16[32,32,1024]{2,1,0:T(8,128)(2,1)}), bf16[32,32,1024]{2,1,0:T(8,128)(2,1)S(1)}, u32[]{:S(2)}, u32[]{:S(2)}) async-start(bf16[32,32,1024]{2,1,0:T(8,128)(2,1)} %bitcast.22), calls=%async_computation.3 | async-start | bytes 4194304 | tf_op jit(solution)/shard_map/all_to_all | solution.py:55
  89.1 42.4 %copy-start = (bf16[32,32,1024]{2,1,0:T(8,128)(2,1)}, bf16[32,32,1024]{2,1,0:T(8,128)(2,1)S(1)}, u32[]{:S(2)}) copy-start(bf16[32,32,1024]{2,1,0:T(8,128)(2,1)S(1)} %all-to-all-done.3) | copy-start | bytes 6291460
  89.1 34.7 %all-to-all-start.6 = ((bf16[32,32,1024]{2,1,0:T(8,128)(2,1)}), bf16[32,32,1024]{2,1,0:T(8,128)(2,1)}, u32[]{:S(2)}, u32[]{:S(2)}) async-start(bf16[32,32,1024]{2,1,0:T(8,128)(2,1)} %bitcast.37), calls=%async_computation.6 | async-start | bytes 4194304 | tf_op jit(solution)/shard_map/all_to_all | solution.py:55
  123.9 34.7 %all-to-all-start = ((bf16[32,32,1024]{2,1,0:T(8,128)(2,1)}), bf16[32,32,1024]{2,1,0:T(8,128)(2,1)}, u32[]{:S(2)}, u32[]{:S(2)}) async-start(bf16[32,32,1024]{2,1,0:T(8,128)(2,1)} %bitcast.7), calls=%async_computation | async-start | bytes 4194304 | tf_op jit(solution)/shard_map/all_to_all | solution.py:55
  128.6 161.1 %all-reduce.4.cloned.1.call-start = ((), (), s32[]{:S(2)}) async-start(), calls=%async_computation.9 | async-start | bytes 12582912 | tf_op jit(solution)/shard_map/psum | solution.py:64
  163.8 0.7 copy-start.1
  192.0 119.7 %all-to-all-start.2 = ((bf16[32,32,1024]{2,1,0:T(8,128)(2,1)}), bf16[32,32,1024]{2,1,0:T(8,128)(2,1)S(1)}, u32[]{:S(2)}, u32[]{:S(2)}) async-start(bf16[32,32,1024]{2,1,0:T(8,128)(2,1)} %subtract_convert_fusion.2), calls=%async_computation.2 | async-start | bytes 4194304 | tf_op jit(solution)/shard_map/all_to_all | solution.py:48
  311.7 37.2 %all-to-all-start.8 = ((bf16[32,32,1024]{2,1,0:T(8,128)(2,1)}), bf16[32,32,1024]{2,1,0:T(8,128)(2,1)}, u32[]{:S(2)}, u32[]{:S(2)}) async-start(bf16[32,32,1024]{2,1,0:T(8,128)(2,1)} %subtract_convert_fusion), calls=%async_computation.8 | async-start | bytes 4194304 | tf_op jit(solution)/shard_map/all_to_all | solution.py:48
  348.9 34.7 %all-to-all-start.5 = ((bf16[32,32,1024]{2,1,0:T(8,128)(2,1)}), bf16[32,32,1024]{2,1,0:T(8,128)(2,1)}, u32[]{:S(2)}, u32[]{:S(2)}) async-start(bf16[32,32,1024]{2,1,0:T(8,128)(2,1)} %subtract_convert_fusion.1), calls=%async_computation.5 | async-start | bytes 4194304 | tf_op jit(solution)/shard_map/all_to_all | solution.py:48
Sparse Core Ops, SparseCore 0:
  164.0 125.7 all-reduce.3
where the time goes:
time: 398 us; the launch traced here: 397 us
  waiting for transfers between devices  212 us (53%)
  local copies, waits for them, and re-layouts  64.6 us (16%)
  starting transfers between devices  45.8 us (12%)
  other arithmetic  33.8 us (8%)
  between operations  14.3 us (4%)
  matrix products  14.1 us (4%)
  blocking collectives  12.1 us (3%)
    psum x1, waiting for transfers between devices, local(): lax.psum(sums.astype(jnp.bfloat16), 'grp').astype(jnp.float32)  93.5 us
    all_to_all x3, waiting for transfers between devices, local(): lax.all_to_all(send_rows, 'list', split_axis=0, concat_axis=0, tiled=True)  68.5 us
    all_to_all x3, waiting for transfers between devices, route_fn(): lax.all_to_all(residual_rows, 'list', split_axis=0, concat_axis=0, tiled=...  39.6 us
    gather x3, local copies, waits for them, and re-layouts, route_fn(): chosen = table[jnp.clip(list_ids, 0, list_dev - 1)]  25.8 us
    all_to_all x3, starting transfers between devices, route_fn(): lax.all_to_all(residual_rows, 'list', split_axis=0, concat_axis=0, tiled=...  16.2 us
    all_to_all x3, starting transfers between devices, local(): lax.all_to_all(send_slots, 'list', split_axis=0, concat_axis=0, tiled=True)  15.1 us
    convert_element_type x3, other arithmetic, route_fn(): residual_rows = (vec_rows.astype(jnp.float32) - chosen).astype(jnp.bfloat16)  15.1 us
    all_to_all x3, starting transfers between devices, local(): lax.all_to_all(send_rows, 'list', split_axis=0, concat_axis=0, tiled=True)  14.4 us
  transfers between devices with their start and end apart: 10, of which 9 were waited for; matrix products, arithmetic and copies ran while one was open for 22% of the time, Pallas kernels for 0%

commit v1 on v0

--- a/solution.py
+++ b/solution.py
@@ -4,6 +4,12 @@
 from jax.sharding import PartitionSpec as P
 
 STEPS = 3
+
+
+def add_all(x, mesh_axis):
+    parts = lax.all_gather(x, mesh_axis, axis=0, tiled=False)
+    result = parts.sum(axis=0)
+    return result
 
 
 def list_sums(slots, rows, list_dev):
@@ -61,7 +67,7 @@
         flat_slots = recv_slots.reshape(-1)
         sums, batch_count = list_sums(flat_slots, flat_rows, list_dev)
         total_sums, total_count = (
-            lax.psum(sums.astype(jnp.bfloat16), "grp").astype(jnp.float32),
+            add_all(sums.astype(jnp.bfloat16), "grp").astype(jnp.float32),
             lax.psum(batch_count.astype(jnp.bfloat16), "grp").astype(jnp.float32),
         )
         current = (weights[:, None] * current + total_sums) / (weights + total_count)[:, None]

time: 398 us -> 448 us (1.13); the launches traced: 397 us -> 439 us
  waiting for transfers between devices: 212 us -> 236 us
  other arithmetic: 33.8 us -> 55.4 us
    all_gather x0 -> x3, waiting for transfers between devices: none -> 102 us  [add_all(): parts = lax.all_gather(x, mesh_axis, axis=0, tiled=False)]
    psum x1 -> x0, waiting for transfers between devices: 93.5 us -> none  [local(): lax.psum(sums.astype(jnp.bfloat16), 'grp').astype(jnp.float32)]
    reduce_sum x0 -> x3, other arithmetic: none -> 22.4 us  [add_all(): result = parts.sum(axis=0)]
    all_to_all x3, waiting for transfers between devices: 68.5 us -> 87 us  [local(): lax.all_to_all(send_rows, 'list', split_axis=0, concat_axis=0, tiled=True)]
  transfers between devices with their start and end apart: 10 -> 12, of which waited for: 9 -> 10; matrix products, arithmetic and copies ran while one was open for 22% -> 25% of each run, Pallas kernels for 0% -> 0%
where the time goes in v1:
time: 448 us; the launch traced here: 439 us
  waiting for transfers between devices  236 us (53%)
  local copies, waits for them, and re-layouts  64.2 us (14%)
  other arithmetic  55.4 us (12%)
  starting transfers between devices  46.5 us (10%)
  between operations  14.5 us (3%)
  blocking collectives  12.1 us (3%)
  matrix products  10.9 us (2%)
    all_gather x3, waiting for transfers between devices, add_all(): parts = lax.all_gather(x, mesh_axis, axis=0, tiled=False)  102 us
    all_to_all x3, waiting for transfers between devices, local(): lax.all_to_all(send_rows, 'list', split_axis=0, concat_axis=0, tiled=True)  87 us
    all_to_all x3, waiting for transfers between devices, route_fn(): lax.all_to_all(residual_rows, 'list', split_axis=0, concat_axis=0, tiled=...  39.5 us
    gather x3, local copies, waits for them, and re-layouts, route_fn(): chosen = table[jnp.clip(list_ids, 0, list_dev - 1)]  25.8 us
    reduce_sum x3, other arithmetic, add_all(): result = parts.sum(axis=0)  22.4 us
    all_to_all x3, starting transfers between devices, route_fn(): lax.all_to_all(residual_rows, 'list', split_axis=0, concat_axis=0, tiled=...  16.5 us
    all_to_all x3, starting transfers between devices, local(): lax.all_to_all(send_slots, 'list', split_axis=0, concat_axis=0, tiled=True)  15.2 us
    all_to_all x3, starting transfers between devices, local(): lax.all_to_all(send_rows, 'list', split_axis=0, concat_axis=0, tiled=True)  14.8 us
  transfers between devices with their start and end apart: 12, of which 10 were waited for; matrix products, arithmetic and copies ran while one was open for 25% of the time, Pallas kernels for 0%

profile of v1, /device:TPU:0, one launch (start us, length us, event | category | flops | bytes accessed | tf_op | source)
XLA Modules:
  0.0 439.3 jit_solution(10190316532154573034)
XLA Ops:
  7.2 0.8 fusion.46
  8.0 0.7 fusion.47
  8.7 1.2 reduce-window.26
  9.9 0.2 slice_reduce_fusion
  10.2 1.2 reduce-window.20
  11.3 0.2 slice_reduce_fusion.2
  11.6 1.2 reduce-window.24
  12.8 0.2 slice_reduce_fusion.1
  13.0 0.1 fusion.29
  13.2 0.1 fusion.35
  13.4 0.7 compare_select_fusion.4
  14.1 2.4 scatter_custom_fusion.5
  16.5 0.7 all_to_all.45
  17.2 7.4 %all-to-all-start.7 = ((s32[32,1,32]{2,1,0:T(1,128)}), s32[32,1,32]{2,1,0:T(1,128)S(1)}, u32[]{:S(2)}, u32[]{:S(2)}) async-start(s32[32,1,32]{2,1,0:T(1,128)} %all_to_all.45), calls=%async_computation.7 | async-start | bytes 32768 | tf_op jit(solution)/shard_map/all_to_all | solution.py:62
  24.6 4.8 %scatter_custom_fusion.4 = bf16[1024,1024]{1,0:T(8,128)(2,1)} fusion(s32[512]{0:T(512)S(1)} %bitcast.160, bf16[3,512,1024]{2,1,0:T(8,128)(2,1)} %param.5, bf16[]{:T(256)} %constant.24.clone.1), kind=kCustom, calls=%fused_computation.37 | custom fusion | bytes 3146240 | tf_op jit(solution)/shard_map/scatter | solution.py:43
  29.4 2.5 all-to-all-done.7
  31.9 4.9 %all-to-all-start.6 = ((bf16[32,32,1024]{2,1,0:T(8,128)(2,1)}), bf16[32,32,1024]{2,1,0:T(8,128)(2,1)S(1)}, u32[]{:S(2)}, u32[]{:S(2)}) async-start(bf16[32,32,1024]{2,1,0:T(8,128)(2,1)} %bitcast.38), calls=%async_computation.6 | async-start | bytes 4194304 | tf_op jit(solution)/shard_map/all_to_all | solution.py:61
  36.9 0.5 broadcast.296
  37.4 0.6 reduce.23
  38.1 28.7 %all-to-all-done.6 = bf16[32,32,1024]{2,1,0:T(8,128)(2,1)S(1)} async-done(((bf16[32,32,1024]{2,1,0:T(8,128)(2,1)}), bf16[32,32,1024]{2,1,0:T(8,128)(2,1)S(1)}, u32[]{:S(2)}, u32[]{:S(2)}) %all-to-all-start.6) | async-done | bytes 2097184 | tf_op jit(solution)/shard_map/all_to_all | solution.py:61
  66.8 3.7 fusion.14
  70.5 2.4 scatter_custom_fusion.3
  73.0 0.7 all_to_all.41
  73.6 3.9 all-to-all-start.4
  77.6 4.9 %scatter_custom_fusion.2 = bf16[1024,1024]{1,0:T(8,128)(2,1)} fusion(s32[512]{0:T(512)S(1)} %bitcast.163, bf16[3,512,1024]{2,1,0:T(8,128)(2,1)} %param.5, bf16[]{:T(256)} %constant.24.clone.1), kind=kCustom, calls=%fused_computation.39 | custom fusion | bytes 3146240 | tf_op jit(solution)/shard_map/scatter | solution.py:43
  82.5 2.5 all-to-all-done.4
  85.0 5.0 %all-to-all-start.3 = ((bf16[32,32,1024]{2,1,0:T(8,128)(2,1)}), bf16[32,32,1024]{2,1,0:T(8,128)(2,1)S(1)}, u32[]{:S(2)}, u32[]{:S(2)}) async-start(bf16[32,32,1024]{2,1,0:T(8,128)(2,1)} %bitcast.22), calls=%async_computation.3 | async-start | bytes 4194304 | tf_op jit(solution)/shard_map/all_to_all | solution.py:61
  90.1 0.6 reduce.21
  90.8 29.2 %all-to-all-done.3 = bf16[32,32,1024]{2,1,0:T(8,128)(2,1)S(1)} async-done(((bf16[32,32,1024]{2,1,0:T(8,128)(2,1)}), bf16[32,32,1024]{2,1,0:T(8,128)(2,1)S(1)}, u32[]{:S(2)}, u32[]{:S(2)}) %all-to-all-start.3) | async-done | bytes 2097184 | tf_op jit(solution)/shard_map/all_to_all | solution.py:61
  120.0 3.7 fusion.13
  123.7 2.4 scatter_custom_fusion.1
  126.1 0.7 all_to_all.37
  126.8 3.8 all-to-all-start.1
  130.6 4.8 %scatter_custom_fusion = bf16[1024,1024]{1,0:T(8,128)(2,1)} fusion(s32[512]{0:T(512)S(1)} %bitcast.166, bf16[3,512,1024]{2,1,0:T(8,128)(2,1)} %param.5, bf16[]{:T(256)} %constant.24.clone.1), kind=kCustom, calls=%fused_computation.41 | custom fusion | bytes 3146240 | tf_op jit(solution)/shard_map/scatter | solution.py:43
  135.5 2.5 all-to-all-done.1
  138.0 4.8 %all-to-all-start = ((bf16[32,32,1024]{2,1,0:T(8,128)(2,1)}), bf16[32,32,1024]{2,1,0:T(8,128)(2,1)S(1)}, u32[]{:S(2)}, u32[]{:S(2)}) async-start(bf16[32,32,1024]{2,1,0:T(8,128)(2,1)} %bitcast.7), calls=%async_computation | async-start | bytes 4194304 | tf_op jit(solution)/shard_map/all_to_all | solution.py:61
  142.9 0.7 fusion.45
  143.7 29.2 %all-to-all-done = bf16[32,32,1024]{2,1,0:T(8,128)(2,1)S(1)} async-done(((bf16[32,32,1024]{2,1,0:T(8,128)(2,1)}), bf16[32,32,1024]{2,1,0:T(8,128)(2,1)S(1)}, u32[]{:S(2)}, u32[]{:S(2)}) %all-to-all-start) | async-done | bytes 2097184 | tf_op jit(solution)/shard_map/all_to_all | solution.py:61
  172.8 3.6 fusion.12
  176.7 8.6 %gather_fusion = f32[1024,1024]{1,0:T(8,128)} fusion(f32[1024,1024]{1,0:T(8,128)} %param.8, s32[1024]{0:T(1024)S(1)} %broadcast_clamp_fusion.2), kind=kCustom, calls=%fused_computation | custom fusion | bytes 8392704 | tf_op jit(solution)/shard_map/gather | solution.py:52
  185.3 0.5 fusion.6
  185.8 0.5 fusion.7
  186.3 0.5 fusion.8
  186.8 12.1 %all-reduce = (bf16[1024]{0:T(1024)(128)(2,1)S(1)}, bf16[1024]{0:T(1024)(128)(2,1)S(1)}, bf16[1024]{0:T(1024)(128)(2,1)S(1)}) all-reduce(bf16[1024]{0:T(1024)(128)(2,1)S(1)} %fusion.6, bf16[1024]{0:T(1024)(128)(2,1)S(1)} %fusion.7, bf16[1024]{0:T(1024)(128)(2,1)S(1)} %fusion.8), channel_id=1, replica_groups=mesh['grp'=4,'list'=32] {'grp'}, use_global_device_ids=true, to_apply=%region_11.12 | all-reduce | flops 3072 | bytes 12288 | tf_op jit(solution)/shard_map/psum | solution.py:71
  198.9 4.4 %subtract_convert_fusion.2 = bf16[32,32,1024]{2,1,0:T(8,128)(2,1)} fusion(f32[32,32,1024]{2,1,0:T(8,128)} %bitcast.136, bf16[32,32,1024]{2,1,0:T(8,128)(2,1)S(1)} %all-to-all-done), kind=kLoop, calls=%fused_computation.26 | loop fusion | flops 3145728 | bytes 8388608 | tf_op jit(solution)/shard_map/convert_element_type | solution.py:53
  203.4 4.2 all-to-all-start.2
  207.6 7.4 %reduce_sum.115 = bf16[1024,1024]{1,0:T(8,128)(2,1)} reduce(bf16[4,1024,1024]{2,1,0:T(8,128)(2,1)} %bitcast.139, bf16[]{:T(256)} %constant.24.clone.1), dimensions={0}, to_apply=%region_21.22 | reduce | flops 3145728 | bytes 10485762 | tf_op jit(solution)/shard_map/reduce_sum | solution.py:11
  215.1 23.3 %all-gather.9.cloned.1.call-done = bf16[4096,1024]{1,0:T(8,128)(2,1)} async-done(((bf16[1024,1024]{1,0:T(8,128)(2,1)}), bf16[4096,1024]{1,0:T(8,128)(2,1)}) %all-gather.9.cloned.1.call-update) | async-done | bytes 8388624 | tf_op jit(solution)/shard_map/all_gather | solution.py:10
  238.4 7.4 %reduce_sum.113 = bf16[1024,1024]{1,0:T(8,128)(2,1)} reduce(bf16[4,1024,1024]{2,1,0:T(8,128)(2,1)} %bitcast.140, bf16[]{:T(256)} %constant.24.clone.1), dimensions={0}, to_apply=%region_17.18 | reduce | flops 3145728 | bytes 10485762 | tf_op jit(solution)/shard_map/reduce_sum | solution.py:11
  245.8 78.2 %all-gather.7.cloned.1.call-done = bf16[4096,1024]{1,0:T(8,128)(2,1)} async-done(((bf16[1024,1024]{1,0:T(8,128)(2,1)}), bf16[4096,1024]{1,0:T(8,128)(2,1)}) %all-gather.7.cloned.1.call-update) | async-done | bytes 8388624 | tf_op jit(solution)/shard_map/all_gather | solution.py:10
  324.0 7.5 %reduce_sum.109 = bf16[1024,1024]{1,0:T(8,128)(2,1)} reduce(bf16[4,1024,1024]{2,1,0:T(8,128)(2,1)} %bitcast.141, bf16[]{:T(256)} %constant.24.clone.1), dimensions={0}, to_apply=%region_9.10 | reduce | flops 3145728 | bytes 10485762 | tf_op jit(solution)/shard_map/reduce_sum | solution.py:11
  331.6 8.4 %add_divide_fusion = (f32[1024,1024]{1,0:T(8,128)}, f32[1024,1024]{1,0:T(8,128)}, f32[1024,1024]{1,0:T(8,128)}) fusion(bf16[1024,1024]{1,0:T(8,128)(2,1)} %reduce_sum.115, f32[1024]{0:T(1024)S(1)} %get-tuple-element.8, f32[1024]{0:T(1024)S(1)} %get-tuple-element.9, bf16[1024,1024]{1,0:T(8,128)(2,1)} %reduce_sum.113, f32[1024]{0:T(1024)S(1)} %get-tuple-element.10, ...), kind=kLoop, calls=%fused_computation.12 | loop fusion | flops 12582912 | bytes 23085056 | tf_op jit(solution)/shard_map/div | solution.py:73
  339.9 8.6 %gather_fusion.4 = f32[1024,1024]{1,0:T(8,128)} fusion(f32[1024,1024]{1,0:T(8,128)} %get-tuple-element.6, s32[1024]{0:T(1024)S(1)} %broadcast_clamp_fusion), kind=kCustom, calls=%fused_computation.4 | custom fusion | bytes 8392704 | tf_op jit(solution)/shard_map/gather | solution.py:52
  348.5 5.0 %subtract_convert_fusion = bf16[32,32,1024]{2,1,0:T(8,128)(2,1)} fusion(f32[32,32,1024]{2,1,0:T(8,128)} %bitcast.137, bf16[32,32,1024]{2,1,0:T(8,128)(2,1)} %copy-done), kind=kLoop, calls=%fused_computation.16 | loop fusion | flops 3145728 | bytes 8388608 | tf_op jit(solution)/shard_map/convert_element_type | solution.py:53
  353.5 7.5 %all-to-all-start.8 = ((bf16[32,32,1024]{2,1,0:T(8,128)(2,1)}), bf16[32,32,1024]{2,1,0:T(8,128)(2,1)}, u32[]{:S(2)}, u32[]{:S(2)}) async-start(bf16[32,32,1024]{2,1,0:T(8,128)(2,1)} %subtract_convert_fusion), calls=%async_computation.8 | async-start | bytes 4194304 | tf_op jit(solution)/shard_map/all_to_all | solution.py:54
  361.1 8.6 %gather_fusion.2 = f32[1024,1024]{1,0:T(8,128)} fusion(f32[1024,1024]{1,0:T(8,128)} %get-tuple-element.7, s32[1024]{0:T(1024)S(1)} %broadcast_clamp_fusion.1), kind=kCustom, calls=%fused_computation.2 | custom fusion | bytes 8392704 | tf_op jit(solution)/shard_map/gather | solution.py:52
  369.7 5.0 %subtract_convert_fusion.1 = bf16[32,32,1024]{2,1,0:T(8,128)(2,1)} fusion(f32[32,32,1024]{2,1,0:T(8,128)} %bitcast.138, bf16[32,32,1024]{2,1,0:T(8,128)(2,1)} %copy-done.1), kind=kLoop, calls=%fused_computation.21 | loop fusion | flops 3145728 | bytes 8388608 | tf_op jit(solution)/shard_map/convert_element_type | solution.py:53
  374.7 16.2 %all-to-all-done.8 = bf16[32,32,1024]{2,1,0:T(8,128)(2,1)} async-done(((bf16[32,32,1024]{2,1,0:T(8,128)(2,1)}), bf16[32,32,1024]{2,1,0:T(8,128)(2,1)}, u32[]{:S(2)}, u32[]{:S(2)}) %all-to-all-start.8) | async-done | bytes 2097184 | tf_op jit(solution)/shard_map/all_to_all | solution.py:54
  391.0 4.8 %all-to-all-start.5 = ((bf16[32,32,1024]{2,1,0:T(8,128)(2,1)}), bf16[32,32,1024]{2,1,0:T(8,128)(2,1)}, u32[]{:S(2)}, u32[]{:S(2)}) async-start(bf16[32,32,1024]{2,1,0:T(8,128)(2,1)} %subtract_convert_fusion.1), calls=%async_computation.5 | async-start | bytes 4194304 | tf_op jit(solution)/shard_map/all_to_all | solution.py:54
  395.8 2.1 gather_fusion.1
  397.8 4.6 %gather_fusion.5 = bf16[512,1024]{1,0:T(8,128)(2,1)S(1)} fusion(bf16[1024,1024]{1,0:T(8,128)(2,1)} %bitcast.45, s32[1024]{0:T(1024)S(1)} %pad_clamp_fusion), kind=kCustom, calls=%fused_computation.5 | custom fusion | bytes 2099200 | tf_op jit(solution)/shard_map/gather | solution.py:65
  402.4 23.3 %all-to-all-done.5 = bf16[32,32,1024]{2,1,0:T(8,128)(2,1)} async-done(((bf16[32,32,1024]{2,1,0:T(8,128)(2,1)}), bf16[32,32,1024]{2,1,0:T(8,128)(2,1)}, u32[]{:S(2)}, u32[]{:S(2)}) %all-to-all-start.5) | async-done | bytes 2097184 | tf_op jit(solution)/shard_map/all_to_all | solution.py:54
  425.7 4.6 %gather_fusion.3 = bf16[512,1024]{1,0:T(8,128)(2,1)S(1)} fusion(bf16[1024,1024]{1,0:T(8,128)(2,1)} %bitcast.29, s32[1024]{0:T(1024)S(1)} %pad_clamp_fusion.1), kind=kCustom, calls=%fused_computation.3 | custom fusion | bytes 2099200 | tf_op jit(solution)/shard_map/gather | solution.py:65
  430.3 2.0 pad_maximum_fusion
  (43 shorter events, 1.0 us)
Async XLA Ops:
  17.2 14.7 %all-to-all-start.7 = ((s32[32,1,32]{2,1,0:T(1,128)}), s32[32,1,32]{2,1,0:T(1,128)S(1)}, u32[]{:S(2)}, u32[]{:S(2)}) async-start(s32[32,1,32]{2,1,0:T(1,128)} %all_to_all.45), calls=%async_computation.7 | async-start | bytes 32768 | tf_op jit(solution)/shard_map/all_to_all | solution.py:62
  31.9 34.9 %all-to-all-start.6 = ((bf16[32,32,1024]{2,1,0:T(8,128)(2,1)}), bf16[32,32,1024]{2,1,0:T(8,128)(2,1)S(1)}, u32[]{:S(2)}, u32[]{:S(2)}) async-start(bf16[32,32,1024]{2,1,0:T(8,128)(2,1)} %bitcast.38), calls=%async_computation.6 | async-start | bytes 4194304 | tf_op jit(solution)/shard_map/all_to_all | solution.py:61
  36.8 170.8 %all-gather.11.cloned.1.call-start = ((), (), s32[]{:S(2)}) async-start(), calls=%async_computation.11 | async-start | bytes 10485760 | tf_op jit(solution)/shard_map/all_gather | solution.py:10
  66.8 3.7 copy-start
  73.6 11.3 %all-to-all-start.4 = ((s32[32,1,32]{2,1,0:T(1,128)}), s32[32,1,32]{2,1,0:T(1,128)S(1)}, u32[]{:S(2)}, u32[]{:S(2)}) async-start(s32[32,1,32]{2,1,0:T(1,128)} %all_to_all.41), calls=%async_computation.4 | async-start | bytes 32768 | tf_op jit(solution)/shard_map/all_to_all | solution.py:62
  85.0 35.0 %all-to-all-start.3 = ((bf16[32,32,1024]{2,1,0:T(8,128)(2,1)}), bf16[32,32,1024]{2,1,0:T(8,128)(2,1)S(1)}, u32[]{:S(2)}, u32[]{:S(2)}) async-start(bf16[32,32,1024]{2,1,0:T(8,128)(2,1)} %bitcast.22), calls=%async_computation.3 | async-start | bytes 4194304 | tf_op jit(solution)/shard_map/all_to_all | solution.py:61
  90.0 148.4 %all-gather.9.cloned.1.call-start = ((), (), s32[]{:S(2)}) async-start(), calls=%async_computation.10 | async-start | bytes 10485760 | tf_op jit(solution)/shard_map/all_gather | solution.py:10
  120.0 3.7 copy-start.1
  126.8 11.2 %all-to-all-start.1 = ((s32[32,1,32]{2,1,0:T(1,128)}), s32[32,1,32]{2,1,0:T(1,128)S(1)}, u32[]{:S(2)}, u32[]{:S(2)}) async-start(s32[32,1,32]{2,1,0:T(1,128)} %all_to_all.37), calls=%async_computation.1 | async-start | bytes 32768 | tf_op jit(solution)/shard_map/all_to_all | solution.py:62
  138.0 34.8 %all-to-all-start = ((bf16[32,32,1024]{2,1,0:T(8,128)(2,1)}), bf16[32,32,1024]{2,1,0:T(8,128)(2,1)S(1)}, u32[]{:S(2)}, u32[]{:S(2)}) async-start(bf16[32,32,1024]{2,1,0:T(8,128)(2,1)} %bitcast.7), calls=%async_computation | async-start | bytes 4194304 | tf_op jit(solution)/shard_map/all_to_all | solution.py:61
  142.9 181.2 %all-gather.7.cloned.1.call-start = ((), (), s32[]{:S(2)}) async-start(), calls=%async_computation.9 | async-start | bytes 10485760 | tf_op jit(solution)/shard_map/all_gather | solution.py:10
  172.8 3.7 copy-start.2
  203.4 150.2 %all-to-all-start.2 = ((bf16[32,32,1024]{2,1,0:T(8,128)(2,1)}), bf16[32,32,1024]{2,1,0:T(8,128)(2,1)S(1)}, u32[]{:S(2)}, u32[]{:S(2)}) async-start(bf16[32,32,1024]{2,1,0:T(8,128)(2,1)} %subtract_convert_fusion.2), calls=%async_computation.2 | async-start | bytes 4194304 | tf_op jit(solution)/shard_map/all_to_all | solution.py:54
  353.5 37.4 %all-to-all-start.8 = ((bf16[32,32,1024]{2,1,0:T(8,128)(2,1)}), bf16[32,32,1024]{2,1,0:T(8,128)(2,1)}, u32[]{:S(2)}, u32[]{:S(2)}) async-start(bf16[32,32,1024]{2,1,0:T(8,128)(2,1)} %subtract_convert_fusion), calls=%async_computation.8 | async-start | bytes 4194304 | tf_op jit(solution)/shard_map/all_to_all | solution.py:54
  391.0 34.7 %all-to-all-start.5 = ((bf16[32,32,1024]{2,1,0:T(8,128)(2,1)}), bf16[32,32,1024]{2,1,0:T(8,128)(2,1)}, u32[]{:S(2)}, u32[]{:S(2)}) async-start(bf16[32,32,1024]{2,1,0:T(8,128)(2,1)} %subtract_convert_fusion.1), calls=%async_computation.5 | async-start | bytes 4194304 | tf_op jit(solution)/shard_map/all_to_all | solution.py:54
Sparse Core Ops, SparseCore 0:
  70.6 81.4 all-gather.10
  153.8 84.4 all-gather.8
  240.0 83.9 all-gather.6
